TPU v7x, 256 devices: a whole 4x4x8 slice. The times are simulated.
256 devices in a mesh: row: 8 (over z), col: 8 (over x, core), sub: 4 (over y).
Axes of the slice: x: 4, y: 4, z: 8, core: 2. Of those that a mesh axis runs over, the one named last changes fastest.
Arguments:
- front_entries: float32 [8192, 8192], P('row', ('col', 'sub')), may hold values from -1 to 4, as said below
- child_blocks: float32 [4, 2048, 2048], P('sub', 'row', 'col'), may hold values from -1 to 2, as said below
- child_map: int32 [4, 16], P('sub'), may hold values from 0 to 63, as said below
Outputs:
- factored: float32 [8192, 8192], P('row', ('col', 'sub'))
Inputs may be any that keep to these rules, and one draw needn't show every extreme that they name: Each row of child_map lists 16 different parent blocks in increasing order and ends with block 63. In natural order front_entries is a symmetric matrix, and the assembled front is positive definite. `child_blocks`: in natural order each child's contribution block is a symmetric matrix.
All inputs are finite; a program needn't handle non-finite values.
Results may differ from a plain program's by a relative error of at most 0.00005.
Values sent between devices are 32-bit elements; how exact they have to be, the bound alone decides.
A program may use at most 128 MiB of HBM per device.

v0:
```python
import jax
import jax.numpy as jnp
from jax import lax
from jax.sharding import PartitionSpec as P

BLK = 128
NPIV = 6
highest = lax.Precision.HIGHEST


def broadcast(value, axis, source):
    kept = jnp.where(lax.axis_index(axis) == source, value, 0).astype(value.dtype)
    return lax.psum(kept, axis)


def lookup(index_table, wanted):
    positions = jnp.arange(index_table.shape[0], dtype=jnp.int32)
    return jnp.sum(jnp.where(wanted[..., None] == positions, index_table, 0), axis=-1)


def body(front_entries, child_blocks, child_map):
    row_count = lax.axis_size("row")
    col_count = lax.axis_size("col")
    sub_count = lax.axis_size("sub")
    row_index = lax.axis_index("row")
    col_index = lax.axis_index("col")
    sub_index = lax.axis_index("sub")
    child_tile = child_blocks[0]
    mapping = child_map[0]
    local_rows = front_entries.shape[0]
    row_blocks = local_rows // BLK
    slot_count = front_entries.shape[1] // BLK
    col_blocks = slot_count * sub_count
    child_rows = child_tile.shape[0] // BLK
    child_cols = child_tile.shape[1] // BLK
    zero_carry = jnp.zeros((row_blocks, BLK, col_blocks, BLK), jnp.float32)
    incoming = lax.all_gather(child_tile[None], ("row", "col"), axis=0, tiled=True)
    piece_count = incoming.shape[0]
    source = jnp.arange(piece_count, dtype=jnp.int32)
    source_row = source // col_count
    source_col = source % col_count
    row_parent = lookup(
        mapping, jnp.arange(child_rows, dtype=jnp.int32)[None, :] * row_count + source_row[:, None]
    )
    col_parent = lookup(
        mapping, jnp.arange(child_cols, dtype=jnp.int32)[None, :] * col_count + source_col[:, None]
    )
    row_target = jnp.where(row_parent % row_count == row_index, row_parent // row_count, row_blocks)
    col_target = jnp.where(col_parent % col_count == col_index, col_parent // col_count, col_blocks)
    tile_stack = incoming.reshape(piece_count, child_rows, BLK, child_cols, BLK).transpose(
        0, 1, 3, 2, 4
    )
    spread_sum = zero_carry.at[row_target[:, :, None], :, col_target[:, None, :], :].add(
        tile_stack, mode="drop"
    )
    spread_sum = spread_sum.reshape(local_rows, col_blocks * BLK)
    summed = lax.psum_scatter(spread_sum, "sub", scatter_dimension=1, tiled=True)
    matrix = front_entries + summed
    row_global = jnp.repeat(jnp.arange(row_blocks, dtype=jnp.int32) * row_count + row_index, BLK)
    col_global = jnp.repeat(
        (sub_index * slot_count + jnp.arange(slot_count, dtype=jnp.int32)) * col_count + col_index,
        BLK,
    )
    for pivot_step in range(NPIV):
        sources_col_slot = pivot_step // col_count % slot_count
        sources_pivot_block = pivot_step // row_count
        col_source = matrix[:, sources_col_slot * BLK : (sources_col_slot + 1) * BLK]
        row_source = matrix[sources_pivot_block * BLK : (sources_pivot_block + 1) * BLK, :]
        root_group = pivot_step % col_count * sub_count + pivot_step // col_count // slot_count
        share_col_panel = broadcast(col_source, ("col", "sub"), root_group)
        pivot_block = pivot_step // row_count
        share_diagonal = share_col_panel[pivot_block * BLK : (pivot_block + 1) * BLK, :]
        share_pivot_row_panel, share_diagonal = (
            broadcast(row_source, "row", pivot_step % row_count),
            broadcast(share_diagonal, "row", pivot_step % row_count),
        )
        pivot_factor = jnp.linalg.cholesky(share_diagonal)
        lower_rows = jax.scipy.linalg.solve_triangular(
            pivot_factor, share_col_panel.T, lower=True
        ).T
        upper_rows = jax.scipy.linalg.solve_triangular(
            pivot_factor, share_pivot_row_panel, lower=True
        )
        left_factor = jnp.where(row_global[:, None] > pivot_step, lower_rows, 0.0)
        right_factor = jnp.where(col_global[None, :] > pivot_step, upper_rows, 0.0)
        factor_column = jnp.where(row_global[:, None] >= pivot_step, lower_rows, 0.0)
        left_factor, right_factor, column = (left_factor, right_factor, factor_column)
        matrix = matrix - jnp.dot(left_factor, right_factor, precision=highest)
        col_slot = pivot_step // col_count % slot_count
        is_owner = (col_index == pivot_step % col_count) & (
            sub_index == pivot_step // col_count // slot_count
        )
        existing = matrix[:, col_slot * BLK : (col_slot + 1) * BLK]
        matrix = matrix.at[:, col_slot * BLK : (col_slot + 1) * BLK].set(
            jnp.where(is_owner, column, existing)
        )
    upper_right = (row_global[:, None] < NPIV) & (col_global[None, :] >= NPIV)
    return jnp.where(upper_right, 0.0, matrix)


def solution(mesh):
    placed = (P("row", ("col", "sub")), P("sub", "row", "col"), P("sub", None))
    return jax.shard_map(
        body, mesh=mesh, in_specs=placed, out_specs=P("row", ("col", "sub")), check_vma=False
    )
```

profile of v0, /device:TPU:2, one launch (start us, length us, event | category | flops | bytes accessed | tf_op | source)
XLA Modules:
  0.0 1576.2 jit_solution(9138514772814132844)
XLA Ops:
  9.0 102.0 %all-gather.2.cloned.1.call-done = f32[64,256,256]{2,1,0:T(8,128)} async-done(((f32[1,256,256]{2,1,0:T(8,128)}), f32[64,256,256]{2,1,0:T(8,128)}) %all-gather.2.cloned.1.call-update) | async-done | bytes 16777232 | tf_op jit(solution)/shard_map/all_gather | solution.py:37
  111.0 20.8 %reshape.466 = f32[64,2,128,2,128]{4,3,2,1,0:T(2,128)} reshape(f32[64,256,256]{2,1,0:T(8,128)} %all-gather.2.cloned.1.call-done) | data formatting | bytes 33554432 | tf_op jit(solution)/shard_map/reshape | solution.py:50
  131.8 12.6 copy.62
  146.9 49.3 %scatter_fusion = f32[8,128,8,128]{3,1,2,0:T(8,128)} fusion(f32[8,128,8,128]{3,1,2,0:T(8,128)} %broadcast_in_dim.231, s32[256]{0:T(256)S(1)} %reshape.468, f32[256,128,128]{2,1,0:T(8,128)} %bitcast.192), kind=kCustom, calls=%fused_computation | custom fusion | flops 4194304 | bytes 50333696 | tf_op jit(solution)/shard_map/scatter-add | solution.py:53
  208.1 48.3 %reduce-scatter.2.cloned.1.call-done = f32[1024,256]{0,1:T(8,128)} async-done(((f32[1024,1024]{0,1:T(8,128)}), f32[1024,256]{0,1:T(8,128)}) %reduce-scatter.2.cloned.1.call-update) | async-done | bytes 1048592 | tf_op jit(solution)/shard_map/reduce_scatter | solution.py:57
  260.1 113.2 %all-reduce.19.cloned.1.call-done = f32[1024,128]{0,1:T(8,128)} async-done(((f32[1024,128]{0,1:T(8,128)}), f32[1024,128]{0,1:T(8,128)}) %all-reduce.19.cloned.1.call-update) | async-done | bytes 524304 | tf_op jit(solution)/shard_map/psum | solution.py:13
  375.1 73.6 %all-reduce.41.cloned.1.call-done = (f32[128,256]{0,1:T(8,128)}, f32[128,128]{0,1:T(8,128)}) async-done(((f32[128,256]{0,1:T(8,128)}, f32[128,128]{0,1:T(8,128)}), (f32[128,256]{0,1:T(8,128)}, f32[128,128]{0,1:T(8,128)})) %all-reduce.41.cloned.1.call-update) | async-done | bytes 196624 | tf_op jit(solution)/shard_map/psum | solution.py:13
  450.4 11.7 cholesky.104
  479.6 111.7 %all-reduce.21.cloned.1.call-done = f32[1024,128]{0,1:T(8,128)} async-done(((f32[1024,128]{0,1:T(8,128)}), f32[1024,128]{0,1:T(8,128)}) %all-reduce.21.cloned.1.call-update) | async-done | bytes 524304 | tf_op jit(solution)/shard_map/psum | solution.py:13
  593.1 73.5 %all-reduce.39.cloned.1.call-done = (f32[128,256]{0,1:T(8,128)}, f32[128,128]{0,1:T(8,128)}) async-done(((f32[128,256]{0,1:T(8,128)}, f32[128,128]{0,1:T(8,128)}), (f32[128,256]{0,1:T(8,128)}, f32[128,128]{0,1:T(8,128)})) %all-reduce.39.cloned.1.call-update) | async-done | bytes 196624 | tf_op jit(solution)/shard_map/psum | solution.py:13
  668.4 11.7 cholesky.115
  697.5 111.7 %all-reduce.23.cloned.1.call-done = f32[1024,128]{0,1:T(8,128)} async-done(((f32[1024,128]{0,1:T(8,128)}), f32[1024,128]{0,1:T(8,128)}) %all-reduce.23.cloned.1.call-update) | async-done | bytes 524304 | tf_op jit(solution)/shard_map/psum | solution.py:13
  811.1 73.6 %all-reduce.37.cloned.1.call-done = (f32[128,256]{0,1:T(8,128)}, f32[128,128]{0,1:T(8,128)}) async-done(((f32[128,256]{0,1:T(8,128)}, f32[128,128]{0,1:T(8,128)}), (f32[128,256]{0,1:T(8,128)}, f32[128,128]{0,1:T(8,128)})) %all-reduce.37.cloned.1.call-update) | async-done | bytes 196624 | tf_op jit(solution)/shard_map/psum | solution.py:13
  886.5 11.7 cholesky.126
  915.7 111.7 %all-reduce.25.cloned.1.call-done = f32[1024,128]{0,1:T(8,128)} async-done(((f32[1024,128]{0,1:T(8,128)}), f32[1024,128]{0,1:T(8,128)}) %all-reduce.25.cloned.1.call-update) | async-done | bytes 524304 | tf_op jit(solution)/shard_map/psum | solution.py:13
  1029.4 73.3 %all-reduce.35.cloned.1.call-done = (f32[128,256]{0,1:T(8,128)}, f32[128,128]{0,1:T(8,128)}) async-done(((f32[128,256]{0,1:T(8,128)}, f32[128,128]{0,1:T(8,128)}), (f32[128,256]{0,1:T(8,128)}, f32[128,128]{0,1:T(8,128)})) %all-reduce.35.cloned.1.call-update) | async-done | bytes 196624 | tf_op jit(solution)/shard_map/psum | solution.py:13
  1104.5 11.7 cholesky.137
  1133.7 111.7 %all-reduce.27.cloned.1.call-done = f32[1024,128]{0,1:T(8,128)} async-done(((f32[1024,128]{0,1:T(8,128)}), f32[1024,128]{0,1:T(8,128)}) %all-reduce.27.cloned.1.call-update) | async-done | bytes 524304 | tf_op jit(solution)/shard_map/psum | solution.py:13
  1247.1 73.6 %all-reduce.33.cloned.1.call-done = (f32[128,256]{0,1:T(8,128)}, f32[128,128]{0,1:T(8,128)}) async-done(((f32[128,256]{0,1:T(8,128)}, f32[128,128]{0,1:T(8,128)}), (f32[128,256]{0,1:T(8,128)}, f32[128,128]{0,1:T(8,128)})) %all-reduce.33.cloned.1.call-update) | async-done | bytes 196624 | tf_op jit(solution)/shard_map/psum | solution.py:13
  1322.5 11.7 cholesky.148
  1335.5 9.8 custom-call.28
  1351.8 111.5 %all-reduce.29.cloned.1.call-done = f32[1024,128]{0,1:T(8,128)} async-done(((f32[1024,128]{0,1:T(8,128)}), f32[1024,128]{0,1:T(8,128)}) %all-reduce.29.cloned.1.call-update) | async-done | bytes 524304 | tf_op jit(solution)/shard_map/psum | solution.py:13
  1464.9 73.8 %all-reduce.31.cloned.1.call-done = (f32[128,256]{0,1:T(8,128)}, f32[128,128]{0,1:T(8,128)}) async-done(((f32[128,256]{0,1:T(8,128)}, f32[128,128]{0,1:T(8,128)}), (f32[128,256]{0,1:T(8,128)}, f32[128,128]{0,1:T(8,128)})) %all-reduce.31.cloned.1.call-update) | async-done | bytes 196624 | tf_op jit(solution)/shard_map/psum | solution.py:13
  1540.5 11.7 cholesky.159
  (157 shorter events, 136.3 us)
Async XLA Ops:
  6.5 104.5 %all-gather.2.cloned.1.call-start = ((), (), s32[]{:S(2)}) async-start(), calls=%async_computation.1 | async-start | bytes 17039360 | tf_op jit(solution)/shard_map/all_gather | solution.py:37
  7.3 249.2 %reduce-scatter.2.cloned.1.call-start = ((), (), s32[]{:S(2)}) async-start(), calls=%async_computation.2 | async-start | bytes 5242880 | tf_op jit(solution)/shard_map/reduce_scatter | solution.py:57
  196.2 10.7 copy-start
  206.9 166.4 %all-reduce.19.cloned.1.call-start = ((), (), s32[]{:S(2)}) async-start(), calls=%async_computation.3 | async-start | bytes 1048576 | tf_op jit(solution)/shard_map/psum | solution.py:13
  258.7 190.0 %all-reduce.41.cloned.1.call-start = ((), (), s32[]{:S(2)}) async-start(), calls=%async_computation.14 | async-start | bytes 393216 | tf_op jit(solution)/shard_map/psum | solution.py:13
  374.8 216.5 %all-reduce.21.cloned.1.call-start = ((), (), s32[]{:S(2)}) async-start(), calls=%async_computation.4 | async-start | bytes 1048576 | tf_op jit(solution)/shard_map/psum | solution.py:13
  478.8 187.8 %all-reduce.39.cloned.1.call-start = ((), (), s32[]{:S(2)}) async-start(), calls=%async_computation.13 | async-start | bytes 393216 | tf_op jit(solution)/shard_map/psum | solution.py:13
  592.7 216.5 %all-reduce.23.cloned.1.call-start = ((), (), s32[]{:S(2)}) async-start(), calls=%async_computation.5 | async-start | bytes 1048576 | tf_op jit(solution)/shard_map/psum | solution.py:13
  696.8 188.0 %all-reduce.37.cloned.1.call-start = ((), (), s32[]{:S(2)}) async-start(), calls=%async_computation.12 | async-start | bytes 393216 | tf_op jit(solution)/shard_map/psum | solution.py:13
  810.7 216.6 %all-reduce.25.cloned.1.call-start = ((), (), s32[]{:S(2)}) async-start(), calls=%async_computation.6 | async-start | bytes 1048576 | tf_op jit(solution)/shard_map/psum | solution.py:13
  914.9 187.8 %all-reduce.35.cloned.1.call-start = ((), (), s32[]{:S(2)}) async-start(), calls=%async_computation.11 | async-start | bytes 393216 | tf_op jit(solution)/shard_map/psum | solution.py:13
  1028.8 216.5 %all-reduce.27.cloned.1.call-start = ((), (), s32[]{:S(2)}) async-start(), calls=%async_computation.7 | async-start | bytes 1048576 | tf_op jit(solution)/shard_map/psum | solution.py:13
  1132.9 187.8 %all-reduce.33.cloned.1.call-start = ((), (), s32[]{:S(2)}) async-start(), calls=%async_computation.10 | async-start | bytes 393216 | tf_op jit(solution)/shard_map/psum | solution.py:13
  1246.8 216.5 %all-reduce.29.cloned.1.call-start = ((), (), s32[]{:S(2)}) async-start(), calls=%async_computation.8 | async-start | bytes 1048576 | tf_op jit(solution)/shard_map/psum | solution.py:13
  1350.8 187.9 %all-reduce.31.cloned.1.call-start = ((), (), s32[]{:S(2)}) async-start(), calls=%async_computation.9 | async-start | bytes 393216 | tf_op jit(solution)/shard_map/psum | solution.py:13
Sparse Core Ops, SparseCore 0:
  10.1 100.8 all-gather.1
  207.0 49.4 reduce-scatter.1
  259.6 113.5 all-reduce.18
  375.5 73.0 all-reduce.40
  478.9 112.2 all-reduce.20
  593.5 73.0 all-reduce.38
  696.9 112.2 all-reduce.22
  811.6 73.0 all-reduce.36
  915.0 112.2 all-reduce.24
  1029.6 73.0 all-reduce.34
  1133.0 112.2 all-reduce.26
  1247.5 73.0 all-reduce.32
  1351.0 112.3 all-reduce.28
  1465.6 73.0 all-reduce.30
where the time goes:
time: 1580 us
  waiting for transfers between devices  1260 us (80%)
  other arithmetic  217 us (14%)
  local copies, waits for them, and re-layouts  55.7 us (4%)
  matrix products  23.1 us (1%)
    psum x12, waiting for transfers between devices, broadcast(): return lax.psum(kept, axis)  1110 us
    all_gather x1, waiting for transfers between devices, body(): lax.all_gather(child_tile[None], ('row', 'col'), axis=0, tiled=True)  102 us
    another operation x18, other arithmetic, body(): pivot_factor = jnp.linalg.cholesky(share_diagonal)  74.3 us
    another operation x12, other arithmetic, body(): jax.scipy.linalg.solve_triangular(pivot_factor, share_col_panel.T, lower=...  62.8 us
    scatter-add x1, other arithmetic, body(): zero_carry.at[row_target[:, :, None], :, col_target[:, None, :], :]  49.3 us
    reduce_scatter x1, waiting for transfers between devices, body(): lax.psum_scatter(spread_sum, 'sub', scatter_dimension=1, tiled=True)  48.3 us
  transfers between devices with their start and end apart: 14, of which 14 were waited for; matrix products, arithmetic and copies ran while one was open for 1% of the time, Pallas kernels for 0%

commit v1 on v0

--- a/solution.py
+++ b/solution.py
@@ -34,7 +34,13 @@
     child_rows = child_tile.shape[0] // BLK
     child_cols = child_tile.shape[1] // BLK
     zero_carry = jnp.zeros((row_blocks, BLK, col_blocks, BLK), jnp.float32)
-    incoming = lax.all_gather(child_tile[None], ("row", "col"), axis=0, tiled=True)
+    keep_up_notes_by_axis = lambda w_in: jnp.concatenate(
+        lax.all_to_all(
+            jnp.stack([w_in for _ in range(lax.axis_size(("row", "col")))]), ("row", "col"), 0, 0
+        ),
+        0,
+    )
+    incoming = keep_up_notes_by_axis(child_tile[None])
     piece_count = incoming.shape[0]
     source = jnp.arange(piece_count, dtype=jnp.int32)
     source_row = source // col_count

time: 1580 us -> 1870 us (1.18)
  waiting for transfers between devices: 1260 us -> 1530 us
    all_to_all x0 -> x1, waiting for transfers between devices: none -> 368 us  [body(): lax.all_to_all(jnp.stack([w_in for _ in range(lax.axis_size(('row', 'col'...]
    all_gather x1 -> x0, waiting for transfers between devices: 102 us -> none  [body(): lax.all_gather(child_tile[None], ('row', 'col'), axis=0, tiled=True)]
    another operation x0 -> x2, local copies, waits for them, and re-layouts: none -> 29.5 us  [the longest x1 20.8 us: body(): incoming.reshape(piece_count, child_rows, BLK, child_cols, BLK)]
    reshape x1 -> x0, local copies, waits for them, and re-layouts: 20.8 us -> none  [body(): incoming.reshape(piece_count, child_rows, BLK, child_cols, BLK)]
  transfers between devices with their start and end apart: 14 -> 14, of which waited for: 14 -> 14; matrix products, arithmetic and copies ran while one was open for 1% -> 0% of each run, Pallas kernels for 0% -> 0%
where the time goes in v1:
time: 1870 us
  waiting for transfers between devices  1530 us (82%)
  other arithmetic  217 us (12%)
  local copies, waits for them, and re-layouts  64.4 us (3%)
  matrix products  23.1 us (1%)
    psum x12, waiting for transfers between devices, broadcast(): return lax.psum(kept, axis)  1110 us
    all_to_all x1, waiting for transfers between devices, body(): lax.all_to_all(jnp.stack([w_in for _ in range(lax.axis_size(('row', 'col'...  368 us
    another operation x18, other arithmetic, body(): pivot_factor = jnp.linalg.cholesky(share_diagonal)  74.3 us
    another operation x12, other arithmetic, body(): jax.scipy.linalg.solve_triangular(pivot_factor, share_col_panel.T, lower=...  62.8 us
    reduce_scatter x1, waiting for transfers between devices, body(): lax.psum_scatter(spread_sum, 'sub', scatter_dimension=1, tiled=True)  51.3 us
    scatter-add x1, other arithmetic, body(): zero_carry.at[row_target[:, :, None], :, col_target[:, None, :], :]  49.3 us
  transfers between devices with their start and end apart: 14, of which 14 were waited for; matrix products, arithmetic and copies ran while one was open for 0% of the time, Pallas kernels for 0%

profile of v1, /device:TPU:2, one launch (start us, length us, event | category | flops | bytes accessed | tf_op | source)
XLA Modules:
  0.0 1865.1 jit_solution(10285731017699056300)
XLA Ops:
  15.2 12.3 all-to-all-start
  28.6 367.7 %all-to-all-done = f32[64,1,256,256]{3,2,1,0:T(8,128)} async-done(((f32[64,1,256,256]{3,2,1,0:T(8,128)}), f32[64,1,256,256]{3,2,1,0:T(8,128)}, u32[]{:S(2)}, u32[]{:S(2)}) %all-to-all-start) | async-done | bytes 16777248 | tf_op jit(solution)/shard_map/all_to_all | solution.py:38
  396.4 20.8 %reshape_reshape.3 = f32[64,2,128,2,128]{4,3,2,1,0:T(2,128)} reshape(f32[64,1,256,256]{3,2,1,0:T(8,128)} %all-to-all-done) | data formatting | bytes 33554432 | tf_op jit(solution)/shard_map/reshape;reshape | solution.py:56
  417.2 12.6 copy.82
  432.2 49.3 %scatter_fusion = f32[8,128,8,128]{3,1,2,0:T(8,128)} fusion(f32[8,128,8,128]{3,1,2,0:T(8,128)} %broadcast_in_dim.231, s32[256]{0:T(256)S(1)} %reshape.467, f32[256,128,128]{2,1,0:T(8,128)} %bitcast.195), kind=kCustom, calls=%fused_computation | custom fusion | flops 4194304 | bytes 50333696 | tf_op jit(solution)/shard_map/scatter-add | solution.py:59
  493.5 51.3 %reduce-scatter.2.cloned.1.call-done = f32[1024,256]{0,1:T(8,128)} async-done(((f32[1024,1024]{0,1:T(8,128)}), f32[1024,256]{0,1:T(8,128)}) %reduce-scatter.2.cloned.1.call-update) | async-done | bytes 1048592 | tf_op jit(solution)/shard_map/reduce_scatter | solution.py:63
  548.4 113.1 %all-reduce.19.cloned.1.call-done = f32[1024,128]{0,1:T(8,128)} async-done(((f32[1024,128]{0,1:T(8,128)}), f32[1024,128]{0,1:T(8,128)}) %all-reduce.19.cloned.1.call-update) | async-done | bytes 524304 | tf_op jit(solution)/shard_map/psum | solution.py:13
  663.3 73.7 %all-reduce.41.cloned.1.call-done = (f32[128,256]{0,1:T(8,128)}, f32[128,128]{0,1:T(8,128)}) async-done(((f32[128,256]{0,1:T(8,128)}, f32[128,128]{0,1:T(8,128)}), (f32[128,256]{0,1:T(8,128)}, f32[128,128]{0,1:T(8,128)})) %all-reduce.41.cloned.1.call-update) | async-done | bytes 196624 | tf_op jit(solution)/shard_map/psum | solution.py:13
  738.9 11.7 cholesky.104
  768.0 111.7 %all-reduce.21.cloned.1.call-done = f32[1024,128]{0,1:T(8,128)} async-done(((f32[1024,128]{0,1:T(8,128)}), f32[1024,128]{0,1:T(8,128)}) %all-reduce.21.cloned.1.call-update) | async-done | bytes 524304 | tf_op jit(solution)/shard_map/psum | solution.py:13
  881.5 73.5 %all-reduce.39.cloned.1.call-done = (f32[128,256]{0,1:T(8,128)}, f32[128,128]{0,1:T(8,128)}) async-done(((f32[128,256]{0,1:T(8,128)}, f32[128,128]{0,1:T(8,128)}), (f32[128,256]{0,1:T(8,128)}, f32[128,128]{0,1:T(8,128)})) %all-reduce.39.cloned.1.call-update) | async-done | bytes 196624 | tf_op jit(solution)/shard_map/psum | solution.py:13
  956.8 11.7 cholesky.115
  985.9 111.7 %all-reduce.23.cloned.1.call-done = f32[1024,128]{0,1:T(8,128)} async-done(((f32[1024,128]{0,1:T(8,128)}), f32[1024,128]{0,1:T(8,128)}) %all-reduce.23.cloned.1.call-update) | async-done | bytes 524304 | tf_op jit(solution)/shard_map/psum | solution.py:13
  1099.5 73.6 %all-reduce.37.cloned.1.call-done = (f32[128,256]{0,1:T(8,128)}, f32[128,128]{0,1:T(8,128)}) async-done(((f32[128,256]{0,1:T(8,128)}, f32[128,128]{0,1:T(8,128)}), (f32[128,256]{0,1:T(8,128)}, f32[128,128]{0,1:T(8,128)})) %all-reduce.37.cloned.1.call-update) | async-done | bytes 196624 | tf_op jit(solution)/shard_map/psum | solution.py:13
  1174.9 11.7 cholesky.126
  1204.1 111.7 %all-reduce.25.cloned.1.call-done = f32[1024,128]{0,1:T(8,128)} async-done(((f32[1024,128]{0,1:T(8,128)}), f32[1024,128]{0,1:T(8,128)}) %all-reduce.25.cloned.1.call-update) | async-done | bytes 524304 | tf_op jit(solution)/shard_map/psum | solution.py:13
  1317.9 73.4 %all-reduce.35.cloned.1.call-done = (f32[128,256]{0,1:T(8,128)}, f32[128,128]{0,1:T(8,128)}) async-done(((f32[128,256]{0,1:T(8,128)}, f32[128,128]{0,1:T(8,128)}), (f32[128,256]{0,1:T(8,128)}, f32[128,128]{0,1:T(8,128)})) %all-reduce.35.cloned.1.call-update) | async-done | bytes 196624 | tf_op jit(solution)/shard_map/psum | solution.py:13
  1393.1 11.7 cholesky.137
  1422.2 111.6 %all-reduce.27.cloned.1.call-done = f32[1024,128]{0,1:T(8,128)} async-done(((f32[1024,128]{0,1:T(8,128)}), f32[1024,128]{0,1:T(8,128)}) %all-reduce.27.cloned.1.call-update) | async-done | bytes 524304 | tf_op jit(solution)/shard_map/psum | solution.py:13
  1535.7 73.7 %all-reduce.33.cloned.1.call-done = (f32[128,256]{0,1:T(8,128)}, f32[128,128]{0,1:T(8,128)}) async-done(((f32[128,256]{0,1:T(8,128)}, f32[128,128]{0,1:T(8,128)}), (f32[128,256]{0,1:T(8,128)}, f32[128,128]{0,1:T(8,128)})) %all-reduce.33.cloned.1.call-update) | async-done | bytes 196624 | tf_op jit(solution)/shard_map/psum | solution.py:13
  1611.2 11.7 cholesky.148
  1640.5 111.5 %all-reduce.29.cloned.1.call-done = f32[1024,128]{0,1:T(8,128)} async-done(((f32[1024,128]{0,1:T(8,128)}), f32[1024,128]{0,1:T(8,128)}) %all-reduce.29.cloned.1.call-update) | async-done | bytes 524304 | tf_op jit(solution)/shard_map/psum | solution.py:13
  1753.6 73.9 %all-reduce.31.cloned.1.call-done = (f32[128,256]{0,1:T(8,128)}, f32[128,128]{0,1:T(8,128)}) async-done(((f32[128,256]{0,1:T(8,128)}, f32[128,128]{0,1:T(8,128)}), (f32[128,256]{0,1:T(8,128)}, f32[128,128]{0,1:T(8,128)})) %all-reduce.31.cloned.1.call-update) | async-done | bytes 196624 | tf_op jit(solution)/shard_map/psum | solution.py:13
  1829.3 11.7 cholesky.159
  (159 shorter events, 153.4 us)
Async XLA Ops:
  15.2 12.5 copy-start.1
  15.2 381.1 %all-to-all-start = ((f32[64,1,256,256]{3,2,1,0:T(8,128)}), f32[64,1,256,256]{3,2,1,0:T(8,128)}, u32[]{:S(2)}, u32[]{:S(2)}) async-start(f32[64,1,256,256]{3,2,1,0:T(8,128)} %stack.3), calls=%async_computation | async-start | bytes 33554432 | tf_op jit(solution)/shard_map/all_to_all | solution.py:38
  27.6 517.2 %reduce-scatter.2.cloned.1.call-start = ((), (), s32[]{:S(2)}) async-start(), calls=%async_computation.2 | async-start | bytes 5242880 | tf_op jit(solution)/shard_map/reduce_scatter | solution.py:63
  481.5 10.7 copy-start
  492.2 169.4 %all-reduce.19.cloned.1.call-start = ((), (), s32[]{:S(2)}) async-start(), calls=%async_computation.3 | async-start | bytes 1048576 | tf_op jit(solution)/shard_map/psum | solution.py:13
  547.0 190.1 %all-reduce.41.cloned.1.call-start = ((), (), s32[]{:S(2)}) async-start(), calls=%async_computation.14 | async-start | bytes 393216 | tf_op jit(solution)/shard_map/psum | solution.py:13
  663.0 216.6 %all-reduce.21.cloned.1.call-start = ((), (), s32[]{:S(2)}) async-start(), calls=%async_computation.4 | async-start | bytes 1048576 | tf_op jit(solution)/shard_map/psum | solution.py:13
  767.2 187.8 %all-reduce.39.cloned.1.call-start = ((), (), s32[]{:S(2)}) async-start(), calls=%async_computation.13 | async-start | bytes 393216 | tf_op jit(solution)/shard_map/psum | solution.py:13
  881.2 216.5 %all-reduce.23.cloned.1.call-start = ((), (), s32[]{:S(2)}) async-start(), calls=%async_computation.5 | async-start | bytes 1048576 | tf_op jit(solution)/shard_map/psum | solution.py:13
  985.2 188.0 %all-reduce.37.cloned.1.call-start = ((), (), s32[]{:S(2)}) async-start(), calls=%async_computation.12 | async-start | bytes 393216 | tf_op jit(solution)/shard_map/psum | solution.py:13
  1099.1 216.6 %all-reduce.25.cloned.1.call-start = ((), (), s32[]{:S(2)}) async-start(), calls=%async_computation.6 | async-start | bytes 1048576 | tf_op jit(solution)/shard_map/psum | solution.py:13
  1203.3 188.0 %all-reduce.35.cloned.1.call-start = ((), (), s32[]{:S(2)}) async-start(), calls=%async_computation.11 | async-start | bytes 393216 | tf_op jit(solution)/shard_map/psum | solution.py:13
  1317.3 216.6 %all-reduce.27.cloned.1.call-start = ((), (), s32[]{:S(2)}) async-start(), calls=%async_computation.7 | async-start | bytes 1048576 | tf_op jit(solution)/shard_map/psum | solution.py:13
  1421.5 187.9 %all-reduce.33.cloned.1.call-start = ((), (), s32[]{:S(2)}) async-start(), calls=%async_computation.10 | async-start | bytes 393216 | tf_op jit(solution)/shard_map/psum | solution.py:13
  1535.4 216.6 %all-reduce.29.cloned.1.call-start = ((), (), s32[]{:S(2)}) async-start(), calls=%async_computation.8 | async-start | bytes 1048576 | tf_op jit(solution)/shard_map/psum | solution.py:13
  1639.5 188.0 %all-reduce.31.cloned.1.call-start = ((), (), s32[]{:S(2)}) async-start(), calls=%async_computation.9 | async-start | bytes 393216 | tf_op jit(solution)/shard_map/psum | solution.py:13
Sparse Core Ops, SparseCore 0:
  492.3 52.4 reduce-scatter.1
  548.0 113.5 all-reduce.18
  663.9 73.0 all-reduce.40
  767.4 112.2 all-reduce.20
  881.9 73.0 all-reduce.38
  985.3 112.2 all-reduce.22
  1100.0 73.0 all-reduce.36
  1203.4 112.2 all-reduce.24
  1318.2 73.0 all-reduce.34
  1421.6 112.2 all-reduce.26
  1536.2 73.0 all-reduce.32
  1639.7 112.2 all-reduce.28
  1754.4 73.0 all-reduce.30
